TPU v7x, 128 devices: a whole 4x4x4 slice. The times are simulated.
128 devices in a mesh: teacher: 4 (over y_hi, core), seq: 32 (over x, y_lo, z).
Axes of the slice: x: 4, y: 4 (y_hi: 2, y_lo: 2; y = y_hi * 2 + y_lo), z: 4, core: 2. Of those that a mesh axis runs over, the one named last changes fastest.
Arguments:
- activations: bfloat16 [20, 2048, 1536], P('teacher', 'seq'), may hold values from -150 to 150
- teacher_maps: bfloat16 [4, 20, 2048, 1536], P('teacher', None, 'seq'), may hold values from -6 to 6
- projection: bfloat16 [4, 1536, 1536], P('teacher', 'seq'), may hold values from -0.625 to 0.625
- dilated_weight: bfloat16 [1536, 3, 768], P('seq'), may hold values from -0.09375 to 0.09375
- pointwise_weight: bfloat16 [768, 1536], P('seq'), may hold values from -0.21875 to 0.21875
Outputs:
- loss_mean: float32 [], replicated
- dilated_grad: float32 [1536, 3, 768], P('seq')
- pointwise_grad: float32 [768, 1536], P('seq')
All inputs are finite; a program needn't handle non-finite values.
Results may differ from a plain program's by a relative error of at most 0.00081.
Values may be sent and summed in bfloat16 or wider, within the bound.
No kernel may reach another device: no remote copies, remote signals or barrier semaphores. Data moves between devices by JAX's collectives and lax.ppermute only.
A program may use at most 128 MiB of HBM per device.

v0:
```python
import jax
import jax.numpy as jnp
from jax import lax
from jax.sharding import PartitionSpec as P

TAP_DILATION = 16
slope_const = 0.7978845608
cubic_const = 0.044715


def padded(block, sides, width):
    for axis, dim in sides:
        count = lax.axis_size(axis)
        forward = [(i, i + 1) for i in range(count - 1)]
        backward = [(target, source) for source, target in forward]
        low = lax.ppermute(
            lax.slice_in_dim(block, block.shape[dim] - width, None, axis=dim), axis, forward
        )
        high = lax.ppermute(lax.slice_in_dim(block, 0, width, axis=dim), axis, backward)
        block = jnp.concatenate([low, block, high], axis=dim)
    return block


def gelu_tanh(value):
    inside = slope_const * (value + cubic_const * value * value * value)
    return 0.5 * value * (1.0 + jnp.tanh(inside))


def gelu_slope(value):
    inside = slope_const * (value + cubic_const * value * value * value)
    tangent = jnp.tanh(inside)
    return 0.5 * (1.0 + tangent) + 0.5 * value * (1.0 - tangent * tangent) * slope_const * (
        1.0 + 3.0 * cubic_const * value * value
    )


def column_product(left, right):
    return lax.dot_general(
        left, right, (((0,), (0,)), ((), ())), preferred_element_type=jnp.float32
    )


def shards(activations, teacher_maps, projection, dilated_weight, pointwise_weight):
    groups = lax.axis_size("teacher")
    ranks = lax.axis_size("seq")
    win_grp, bins_per_device, channel_count = activations.shape
    branch_width = dilated_weight.shape[2]
    count_of_rows = win_grp * bins_per_device
    total_rows = count_of_rows * groups * ranks
    maps_flat = teacher_maps[0].reshape(-1, teacher_maps.shape[3])
    columns = maps_flat
    projected = jnp.dot(
        columns,
        lax.all_gather(projection, "seq", axis=1, tiled=True)[0],
        preferred_element_type=jnp.float32,
    )
    projected = lax.optimization_barrier(projected.astype(jnp.bfloat16)).astype(jnp.float32)
    summed = lax.psum(projected, "teacher")
    own_rows = lax.dynamic_slice_in_dim(
        summed, lax.axis_index("teacher") * count_of_rows, count_of_rows, 0
    )
    target = own_rows / groups
    inputs_f = activations.reshape(count_of_rows, channel_count).astype(jnp.float32)
    sum_first, sum_second = lax.psum(
        (jnp.sum(inputs_f, axis=0), jnp.sum(inputs_f * inputs_f, axis=0)), ("teacher", "seq")
    )
    channel_mean = sum_first / total_rows
    channel_var = sum_second / total_rows - channel_mean * channel_mean
    normed = (inputs_f - channel_mean) * lax.rsqrt(channel_var + 1e-05)
    hidden_state = (
        gelu_tanh(normed).astype(jnp.bfloat16).reshape(win_grp, bins_per_device, channel_count)
    )
    padded_input = padded(hidden_state, (("seq", 1),), TAP_DILATION)
    tap_weights = [
        padded_input[
            :, offset_index * TAP_DILATION : offset_index * TAP_DILATION + bins_per_device
        ].reshape(count_of_rows, channel_count)
        for offset_index in range(3)
    ]
    running = jnp.zeros((count_of_rows, branch_width), jnp.float32)
    section = lax.all_gather(dilated_weight, "seq", axis=0, tiled=True)
    for offset_index in range(3):
        columns = tap_weights[offset_index]
        running = running + jnp.dot(
            columns, section[:, offset_index, :], preferred_element_type=jnp.float32
        )
    activated = gelu_tanh(running).astype(jnp.bfloat16)
    pointwise_full = lax.all_gather(pointwise_weight, "seq", axis=0, tiled=True)
    student = inputs_f + jnp.dot(activated, pointwise_full, preferred_element_type=jnp.float32)
    misfit = student - target
    squared_total = lax.psum(jnp.sum(misfit * misfit), ("teacher", "seq"))
    loss_mean = 0.5 * squared_total / (channel_count * total_rows)
    out_grad = (misfit / channel_count).astype(jnp.bfloat16)
    back_grad = lax.dot_general(
        out_grad, pointwise_full, (((1,), (1,)), ((), ())), preferred_element_type=jnp.float32
    )
    preact_grad = (back_grad * gelu_slope(running)).astype(jnp.bfloat16)
    dilated_part = lax.psum_scatter(
        jnp.stack(
            [column_product(tap_weights[offset_index], preact_grad) for offset_index in range(3)],
            axis=1,
        ),
        "seq",
        scatter_dimension=0,
        tiled=True,
    )
    pointwise_part = lax.psum_scatter(
        column_product(activated, out_grad), "seq", scatter_dimension=0, tiled=True
    )
    dilated_grad, pointwise_grad = lax.psum((dilated_part, pointwise_part), "teacher")
    return (loss_mean, dilated_grad, pointwise_grad)


def solution(mesh):
    in_specs = (
        P("teacher", "seq", None),
        P("teacher", None, "seq", None),
        P("teacher", "seq", None),
        P("seq", None, None),
        P("seq", None),
    )
    out_specs = (P(), P("seq", None, None), P("seq", None))
    return jax.shard_map(shards, mesh=mesh, in_specs=in_specs, out_specs=out_specs, check_vma=False)
```

profile of v0, /device:TPU:1, one launch (start us, length us, event | category | flops | bytes accessed | tf_op | source)
XLA Modules:
  0.0 940.9 jit_solution(16138648876742079881)
XLA Ops:
  7.2 0.0 copy-start
  7.2 0.0 all-gather.8.cloned.1.call-start
  7.2 0.7 all-gather.8.cloned.1.call-update
  7.9 0.0 all-gather.4.cloned.1.call-start
  8.0 0.7 all-gather.4.cloned.1.call-update
  8.7 0.0 all-gather.6.cloned.1.call-start
  8.7 1.5 convert_reduce_fusion
  10.2 71.5 %all-reduce = (f32[1536]{0:T(1024)S(1)}, f32[1536]{0:T(1024)S(1)}) all-reduce(f32[1536]{0:T(1024)S(1)} %get-tuple-element.4, f32[1536]{0:T(1024)S(1)} %get-tuple-element.3), channel_id=1, replica_groups=mesh['teacher'=4,'seq'=32] {'teacher','seq'}, use_global_device_ids=true, to_apply=%region_3.0 | all-reduce | flops 3072 | bytes 24576 | tf_op jit(solution)/shard_map/psum | solution.py:64
  81.7 0.0 copy-done
  81.7 0.8 fusion.9
  82.6 1.3 collective-permute-start
  83.9 1.3 collective-permute-start.1
  85.2 0.0 all-gather.6.cloned.1.call-update
  85.2 0.0 reduce-scatter.5.cloned.1.call-start
  85.3 5.7 collective-permute-done
  91.0 4.3 collective-permute-done.1
  95.2 1.2 pad_maximum_fusion.2
  96.4 0.0 copy-start.3
  96.4 54.6 %all-gather.8.cloned.1.call-done = bf16[1,1536,1536]{2,1,0:T(8,128)(2,1)} async-done(((bf16[1,48,1536]{2,1,0:T(8,128)(2,1)}), bf16[1,1536,1536]{2,1,0:T(8,128)(2,1)}) %all-gather.8.cloned.1.call-update) | async-done | bytes 4718608 | tf_op jit(solution)/shard_map/all_gather | solution.py:54
  151.0 10.7 %convolution_convert_fusion = bf16[1280,1536]{1,0:T(8,128)(2,1)} fusion(bf16[1280,1536]{1,0:T(8,128)(2,1)} %bitcast.55, bf16[1,1536,1536]{2,1,0:T(8,128)(2,1)} %all-gather.8.cloned.1.call-done), kind=kOutput, calls=%fused_computation.1 | convolution fusion | flops 6041763840 | bytes 12582912 | tf_op jit(solution)/shard_map/dot_general | solution.py:52
  161.7 239.2 %all-reduce.6 = f32[1280,1536]{1,0:T(8,128)} all-reduce(bf16[1280,1536]{1,0:T(8,128)(2,1)} %convolution_convert_fusion), channel_id=1, replica_groups=mesh['teacher'=4,'seq'=32] {'teacher'}, use_global_device_ids=true, to_apply=%region_4.0 | all-reduce | flops 1966080 | bytes 11796480 | tf_op jit(solution)/shard_map/psum | solution.py:58
  400.9 0.0 all-gather.4.cloned.1.call-done
  400.9 0.0 copy-start.5
  400.9 2.7 fusion.3
  403.6 0.0 copy-done.5
  403.6 2.6 fusion.2
  406.2 0.0 copy-done.3
  406.2 3.6 fusion.21
  409.8 60.0 %all-gather.6.cloned.1.call-done = bf16[768,1536]{1,0:T(8,128)(2,1)} async-done(((bf16[24,1536]{1,0:T(8,128)(2,1)}), bf16[768,1536]{1,0:T(8,128)(2,1)}) %all-gather.6.cloned.1.call-update) | async-done | bytes 2359312 | tf_op jit(solution)/shard_map/all_gather | solution.py:88
  469.8 0.0 copy-start.1
  469.8 4.4 multiply_reduce_fusion
  474.2 0.0 copy-done.1
  474.2 3.7 fusion.28
  477.9 0.0 reduce-scatter.5.cloned.1.call-update
  478.0 0.2 reduce-scatter.3.cloned.1.call-start
  478.2 0.0 copy-start.2
  478.2 0.8 fusion.14
  479.0 0.4 copy-done.2
  479.4 0.0 copy-start.6
  479.4 3.0 fusion.22
  482.4 0.0 copy-done.6
  482.4 0.0 copy-start.4
  482.4 3.6 convolution_bitcast_fusion
  486.0 0.0 copy-done.4
  486.0 3.6 convolution_bitcast_fusion.2
  489.6 3.7 convolution_bitcast_fusion.1
  493.3 11.1 %pad_maximum_fusion = f32[1536,3,768]{2,0,1:T(8,128)} fusion(f32[1536,1,768]{2,0,1:T(8,128)} %convolution_bitcast_fusion, f32[1536,1,768]{2,0,1:T(8,128)} %convolution_bitcast_fusion.1, f32[1536,1,768]{2,0,1:T(8,128)} %convolution_bitcast_fusion.2), kind=kLoop, calls=%fused_computation | loop fusion | flops 7077888 | bytes 28311552 | tf_op jit(solution)/shard_map/stack | solution.py:99
  504.3 0.0 reduce-scatter.3.cloned.1.call-update
  504.3 0.0 all-reduce.5.cloned.1.call-start
  504.4 145.1 %reduce-scatter.5.cloned.1.call-done = f32[24,1536]{1,0:T(8,128)} async-done(((f32[768,1536]{1,0:T(8,128)}), f32[24,1536]{1,0:T(8,128)}) %reduce-scatter.5.cloned.1.call-update) | async-done | bytes 147472 | tf_op jit(solution)/shard_map/reduce_scatter | solution.py:107
  649.5 194.7 %reduce-scatter.3.cloned.1.call-done = f32[48,3,768]{2,0,1:T(8,128)} async-done(((f32[1536,3,768]{2,0,1:T(8,128)}), f32[48,3,768]{2,0,1:T(8,128)}) %reduce-scatter.3.cloned.1.call-update) | async-done | bytes 442384 | tf_op jit(solution)/shard_map/reduce_scatter | solution.py:98
  844.2 0.0 all-reduce.5.cloned.1.call-update
  844.2 84.7 %psum.45 = f32[]{:T(128)} all-reduce(f32[]{:T(128)} %get-tuple-element.15), channel_id=1, replica_groups=mesh['teacher'=4,'seq'=32] {'teacher','seq'}, use_global_device_ids=true, to_apply=%region_6.0 | all-reduce | flops 1 | bytes 8 | tf_op jit(solution)/shard_map/psum | solution.py:91
  929.6 0.0 all-reduce.5.cloned.1.call-done
  929.6 1.8 copy.12
  931.4 1.6 copy.13
  (2 shorter events, 0.0 us)
Async XLA Ops:
  7.2 74.5 %copy-start = (bf16[5,64,1536]{2,1,0:T(8,128)(2,1)S(1)}, bf16[5,64,1536]{2,1,0:T(8,128)(2,1)}, u32[]{:S(2)}) copy-start(bf16[5,64,1536]{2,1,0:T(8,128)(2,1)} %param.5) | copy-start | bytes 2949124
  7.2 143.8 %all-gather.8.cloned.1.call-start = ((), (), s32[]{:S(2)}) async-start(), calls=%async_computation.4 | async-start | bytes 4866048 | tf_op jit(solution)/shard_map/all_gather | solution.py:54
  7.9 393.0 %all-gather.4.cloned.1.call-start = ((), (), s32[]{:S(2)}) async-start(), calls=%async_computation.2 | async-start | bytes 7299072 | tf_op jit(solution)/shard_map/all_gather | solution.py:81
  8.7 461.1 %all-gather.6.cloned.1.call-start = ((), (), s32[]{:S(2)}) async-start(), calls=%async_computation.3 | async-start | bytes 2433024 | tf_op jit(solution)/shard_map/all_gather | solution.py:88
  82.6 8.4 collective-permute-start
  83.9 11.4 %collective-permute-start.1 = (bf16[5,16,1536]{2,1,0:T(8,128)(2,1)S(1)}, bf16[5,16,1536]{2,1,0:T(8,128)(2,1)S(1)}, u32[]{:S(2)}, u32[]{:S(2)}) collective-permute-start(bf16[5,16,1536]{2,1,0:T(8,128)(2,1)S(1)} %get-tuple-element.12), channel_id=1, source_target_pairs={{1,0},{2,1},{3,2},{4,3},{5,4},{6,5},{7,6},{8,7},{9,8},{10,9},{11,1... | collective-permute-start | bytes 737288 | tf_op jit(solution)/shard_map/ppermute | solution.py:19
  85.2 564.3 %reduce-scatter.5.cloned.1.call-start = ((), (), s32[]{:S(2)}) async-start(), calls=%async_computation.6 | async-start | bytes 4866048 | tf_op jit(solution)/shard_map/reduce_scatter | solution.py:107
  96.4 309.8 %copy-start.3 = (bf16[5,64,1536]{2,1,0:T(8,128)(2,1)}, bf16[5,64,1536]{2,1,0:T(8,128)(2,1)S(1)}, u32[]{:S(2)}) copy-start(bf16[5,64,1536]{2,1,0:T(8,128)(2,1)S(1)} %get-tuple-element.9) | copy-start | bytes 2949124
  400.9 2.7 copy-start.5
  469.8 4.4 copy-start.1
  478.0 366.2 %reduce-scatter.3.cloned.1.call-start = ((), (), s32[]{:S(2)}) async-start(), calls=%async_computation.5 | async-start | bytes 14598144 | tf_op jit(solution)/shard_map/reduce_scatter | solution.py:98
  478.2 1.2 copy-start.2
  479.4 3.0 copy-start.6
  482.4 3.6 copy-start.4
  504.3 425.2 %all-reduce.5.cloned.1.call-start = ((), (), s32[]{:S(2)}) async-start(), calls=%async_computation.7 | async-start | bytes 1179648 | tf_op jit(solution)/shard_map/psum | solution.py:110
Sparse Core Ops, SparseCore 0:
  9.6 141.3 all-gather.7
  152.6 172.9 all-gather.3
  327.3 142.4 all-gather.5
  478.1 171.3 reduce-scatter.4
  651.8 192.3 reduce-scatter.2
  846.6 61.8 all-reduce.4
where the time goes:
time: 941 us
  waiting for transfers between devices  466 us (50%)
  blocking collectives  395 us (42%)
  matrix products  41.5 us (4%)
  between operations  16 us (2%)
  other arithmetic  15.3 us (2%)
    psum x1, blocking collectives, shards(): summed = lax.psum(projected, 'teacher')  239 us
    reduce_scatter x1, waiting for transfers between devices, shards(): lax.psum_scatter(jnp.stack([column_product(tap_weights[offset_index], pre...  195 us
    reduce_scatter x1, waiting for transfers between devices, shards(): lax.psum_scatter(column_product(activated, out_grad), 'seq', scatter_dime...  145 us
    psum x1, blocking collectives, shards(): squared_total = lax.psum(jnp.sum(misfit * misfit), ('teacher', 'seq'))  84.7 us
    psum x1, blocking collectives, shards(): lax.psum((jnp.sum(inputs_f, axis=0), jnp.sum(inputs_f * inputs_f, axis=0)...  71.5 us
    all_gather x1, waiting for transfers between devices, shards(): pointwise_full = lax.all_gather(pointwise_weight, 'seq', axis=0, tiled=True)  60 us
    all_gather x1, waiting for transfers between devices, shards(): lax.all_gather(projection, 'seq', axis=1, tiled=True)[0]  54.6 us
  transfers between devices with their start and end apart: 8, of which 6 were waited for; matrix products, arithmetic and copies ran while one was open for 5% of the time, Pallas kernels for 0%

commit v1 on v0

--- a/solution.py
+++ b/solution.py
@@ -41,6 +41,10 @@
 
 
 def shards(activations, teacher_maps, projection, dilated_weight, pointwise_weight):
+
+    def process_chains(unit):
+        return jnp.sum(lax.all_gather(unit, "teacher"), 0)
+
     groups = lax.axis_size("teacher")
     ranks = lax.axis_size("seq")
     win_grp, bins_per_device, channel_count = activations.shape
@@ -55,7 +59,7 @@
         preferred_element_type=jnp.float32,
     )
     projected = lax.optimization_barrier(projected.astype(jnp.bfloat16)).astype(jnp.float32)
-    summed = lax.psum(projected, "teacher")
+    summed = process_chains(projected)
     own_rows = lax.dynamic_slice_in_dim(
         summed, lax.axis_index("teacher") * count_of_rows, count_of_rows, 0
     )

time: 941 us -> 1140 us (1.21)
  waiting for transfers between devices: 466 us -> 864 us
  blocking collectives: 395 us -> 173 us
  other arithmetic: 15.3 us -> 33.8 us
    psum x1 -> x0, blocking collectives: 239 us -> none  [shards(): summed = lax.psum(projected, 'teacher')]
    all_gather x0 -> x1, waiting for transfers between devices: none -> 207 us  [process_chains(): return jnp.sum(lax.all_gather(unit, 'teacher'), 0)]
    all_gather x1, waiting for transfers between devices: 54.6 us -> 141 us  [shards(): lax.all_gather(projection, 'seq', axis=1, tiled=True)[0]]
    all_gather x1, waiting for transfers between devices: 60 us -> 117 us  [shards(): pointwise_full = lax.all_gather(pointwise_weight, 'seq', axis=0, tiled=True)]
    all_gather x1, waiting for transfers between devices: 0.01 us -> 44.4 us  [shards(): section = lax.all_gather(dilated_weight, 'seq', axis=0, tiled=True)]
    psum x1, blocking collectives: 71.5 us -> 89.9 us  [shards(): lax.psum((jnp.sum(inputs_f, axis=0), jnp.sum(inputs_f * inputs_f, axis=0)...]
    reduce_sum x0 -> x1, other arithmetic: none -> 15.5 us  [process_chains(): return jnp.sum(lax.all_gather(unit, 'teacher'), 0)]
  transfers between devices with their start and end apart: 8 -> 9, of which waited for: 6 -> 8; matrix products, arithmetic and copies ran while one was open for 5% -> 5% of each run, Pallas kernels for 0% -> 0%
where the time goes in v1:
time: 1140 us
  waiting for transfers between devices  864 us (76%)
  blocking collectives  173 us (15%)
  matrix products  40.3 us (4%)
  other arithmetic  33.8 us (3%)
  between operations  16 us (1%)
    all_gather x1, waiting for transfers between devices, process_chains(): return jnp.sum(lax.all_gather(unit, 'teacher'), 0)  207 us
    reduce_scatter x1, waiting for transfers between devices, shards(): lax.psum_scatter(jnp.stack([column_product(tap_weights[offset_index], pre...  197 us
    reduce_scatter x1, waiting for transfers between devices, shards(): lax.psum_scatter(column_product(activated, out_grad), 'seq', scatter_dime...  144 us
    all_gather x1, waiting for transfers between devices, shards(): lax.all_gather(projection, 'seq', axis=1, tiled=True)[0]  141 us
    all_gather x1, waiting for transfers between devices, shards(): pointwise_full = lax.all_gather(pointwise_weight, 'seq', axis=0, tiled=True)  117 us
    psum x1, blocking collectives, shards(): lax.psum((jnp.sum(inputs_f, axis=0), jnp.sum(inputs_f * inputs_f, axis=0)...  89.9 us
    psum x1, blocking collectives, shards(): squared_total = lax.psum(jnp.sum(misfit * misfit), ('teacher', 'seq'))  83.4 us
    all_gather x1, waiting for transfers between devices, shards(): section = lax.all_gather(dilated_weight, 'seq', axis=0, tiled=True)  44.4 us
  transfers between devices with their start and end apart: 9, of which 8 were waited for; matrix products, arithmetic and copies ran while one was open for 5% of the time, Pallas kernels for 0%

profile of v1, /device:TPU:1, one launch (start us, length us, event | category | flops | bytes accessed | tf_op | source)
XLA Modules:
  0.0 1135.7 jit_solution(12413517175812367093)
XLA Ops:
  7.2 0.0 all-gather.10.cloned.1.call-start
  7.2 0.7 all-gather.10.cloned.1.call-update
  7.9 0.0 all-gather.6.cloned.1.call-start
  7.9 0.7 all-gather.6.cloned.1.call-update
  8.6 0.0 all-gather.12.cloned.1.call-start
  8.7 141.5 %all-gather.10.cloned.1.call-done = bf16[1,1536,1536]{2,1,0:T(8,128)(2,1)} async-done(((bf16[1,48,1536]{2,1,0:T(8,128)(2,1)}), bf16[1,1536,1536]{2,1,0:T(8,128)(2,1)}) %all-gather.10.cloned.1.call-update) | async-done | bytes 4718608 | tf_op jit(solution)/shard_map/all_gather | solution.py:58
  150.1 9.3 convolution_convert_fusion
  159.5 4.2 all_gather.24
  163.7 0.0 copy-start
  163.7 0.0 all-gather.12.cloned.1.call-update
  163.7 0.0 all-gather.8.cloned.1.call-start
  163.8 0.5 all-gather.8.cloned.1.call-update
  164.3 0.0 reduce-scatter.5.cloned.1.call-start
  164.3 0.6 copy-done
  164.9 0.3 convert_reduce_fusion
  165.2 89.9 %all-reduce = (f32[1536]{0:T(1024)S(1)}, f32[1536]{0:T(1024)S(1)}) all-reduce(f32[1536]{0:T(1024)S(1)} %get-tuple-element.4, f32[1536]{0:T(1024)S(1)} %get-tuple-element.3), channel_id=1, replica_groups=mesh['teacher'=4,'seq'=32] {'teacher','seq'}, use_global_device_ids=true, to_apply=%region_3.0 | all-reduce | flops 3072 | bytes 24576 | tf_op jit(solution)/shard_map/psum | solution.py:68
  255.1 0.8 fusion.9
  256.0 2.3 collective-permute-start
  258.3 1.3 collective-permute-start.1
  259.6 6.9 collective-permute-done
  266.5 4.3 collective-permute-done.1
  270.8 1.1 pad_maximum_fusion.2
  272.0 0.0 copy-start.3
  272.0 44.4 %all-gather.6.cloned.1.call-done = bf16[1536,3,768]{2,0,1:T(8,128)(2,1)} async-done(((bf16[48,3,768]{2,0,1:T(8,128)(2,1)}), bf16[1536,3,768]{2,0,1:T(8,128)(2,1)}) %all-gather.6.cloned.1.call-update) | async-done | bytes 7077904 | tf_op jit(solution)/shard_map/all_gather | solution.py:85
  316.3 2.9 fusion.2
  319.2 2.6 fusion.3
  321.8 0.0 copy-done.3
  321.8 3.6 fusion.21
  325.4 207.0 %all-gather.12.cloned.1.call-done = f32[5120,1536]{1,0:T(8,128)} async-done(((f32[1280,1536]{1,0:T(8,128)}), f32[5120,1536]{1,0:T(8,128)}) %all-gather.12.cloned.1.call-update) | async-done | bytes 31457296 | tf_op jit(solution)/shard_map/all_gather | solution.py:46
  532.4 15.5 %reduce_sum.38 = f32[1280,1536]{1,0:T(8,128)} reduce(f32[4,1280,1536]{2,1,0:T(8,128)} %bitcast.50, f32[]{:T(128)} %constant.16.clone.1), dimensions={0}, to_apply=%region_4.0 | reduce | flops 5898240 | bytes 39321604 | tf_op jit(solution)/shard_map/reduce_sum | solution.py:46
  547.9 116.8 %all-gather.8.cloned.1.call-done = bf16[768,1536]{1,0:T(8,128)(2,1)} async-done(((bf16[24,1536]{1,0:T(8,128)(2,1)}), bf16[768,1536]{1,0:T(8,128)(2,1)}) %all-gather.8.cloned.1.call-update) | async-done | bytes 2359312 | tf_op jit(solution)/shard_map/all_gather | solution.py:92
  664.7 0.0 copy-start.1
  664.7 4.4 multiply_reduce_fusion
  669.1 0.0 copy-done.1
  669.1 3.7 fusion.28
  672.8 0.0 reduce-scatter.5.cloned.1.call-update
  672.9 0.2 reduce-scatter.3.cloned.1.call-start
  673.1 0.0 copy-start.2
  673.1 0.8 fusion.14
  673.9 0.4 copy-done.2
  674.3 0.0 copy-start.5
  674.3 3.0 fusion.22
  677.3 0.0 copy-done.5
  677.3 0.0 copy-start.4
  677.4 3.6 convolution_bitcast_fusion
  681.0 0.0 copy-done.4
  681.0 3.5 convolution_bitcast_fusion.2
  684.5 3.6 convolution_bitcast_fusion.1
  688.2 11.1 pad_maximum_fusion
  699.2 0.0 reduce-scatter.3.cloned.1.call-update
  699.2 0.0 all-reduce.4.cloned.1.call-start
  699.3 144.0 %reduce-scatter.5.cloned.1.call-done = f32[24,1536]{1,0:T(8,128)} async-done(((f32[768,1536]{1,0:T(8,128)}), f32[24,1536]{1,0:T(8,128)}) %reduce-scatter.5.cloned.1.call-update) | async-done | bytes 147472 | tf_op jit(solution)/shard_map/reduce_scatter | solution.py:111
  843.3 196.9 %reduce-scatter.3.cloned.1.call-done = f32[48,3,768]{2,0,1:T(8,128)} async-done(((f32[1536,3,768]{2,0,1:T(8,128)}), f32[48,3,768]{2,0,1:T(8,128)}) %reduce-scatter.3.cloned.1.call-update) | async-done | bytes 442384 | tf_op jit(solution)/shard_map/reduce_scatter | solution.py:102
  1040.2 0.0 all-reduce.4.cloned.1.call-update
  1040.2 83.4 %psum.37 = f32[]{:T(128)} all-reduce(f32[]{:T(128)} %get-tuple-element.15), channel_id=1, replica_groups=mesh['teacher'=4,'seq'=32] {'teacher','seq'}, use_global_device_ids=true, to_apply=%region_6.0 | all-reduce | flops 1 | bytes 8 | tf_op jit(solution)/shard_map/psum | solution.py:95
  1124.3 0.0 all-reduce.4.cloned.1.call-done
  1124.3 1.8 copy.10
  1126.1 1.6 copy.11
  (2 shorter events, 0.0 us)
Async XLA Ops:
  7.2 143.0 %all-gather.10.cloned.1.call-start = ((), (), s32[]{:S(2)}) async-start(), calls=%async_computation.4 | async-start | bytes 4866048 | tf_op jit(solution)/shard_map/all_gather | solution.py:58
  7.9 308.4 %all-gather.6.cloned.1.call-start = ((), (), s32[]{:S(2)}) async-start(), calls=%async_computation.2 | async-start | bytes 7299072 | tf_op jit(solution)/shard_map/all_gather | solution.py:85
  8.6 523.8 %all-gather.12.cloned.1.call-start = ((), (), s32[]{:S(2)}) async-start(), calls=%async_computation.7 | async-start | bytes 39321600 | tf_op jit(solution)/shard_map/all_gather | solution.py:46
  163.7 1.2 copy-start
  163.7 501.0 %all-gather.8.cloned.1.call-start = ((), (), s32[]{:S(2)}) async-start(), calls=%async_computation.3 | async-start | bytes 2433024 | tf_op jit(solution)/shard_map/all_gather | solution.py:92
  164.3 679.0 %reduce-scatter.5.cloned.1.call-start = ((), (), s32[]{:S(2)}) async-start(), calls=%async_computation.6 | async-start | bytes 4866048 | tf_op jit(solution)/shard_map/reduce_scatter | solution.py:111
  256.0 10.5 collective-permute-start
  258.3 12.6 %collective-permute-start.1 = (bf16[5,16,1536]{2,1,0:T(8,128)(2,1)S(1)}, bf16[5,16,1536]{2,1,0:T(8,128)(2,1)S(1)}, u32[]{:S(2)}, u32[]{:S(2)}) collective-permute-start(bf16[5,16,1536]{2,1,0:T(8,128)(2,1)S(1)} %get-tuple-element.12), channel_id=1, source_target_pairs={{1,0},{2,1},{3,2},{4,3},{5,4},{6,5},{7,6},{8,7},{9,8},{10,9},{11,1... | collective-permute-start | bytes 737288 | tf_op jit(solution)/shard_map/ppermute | solution.py:19
  272.0 49.9 %copy-start.3 = (bf16[5,64,1536]{2,1,0:T(8,128)(2,1)}, bf16[5,64,1536]{2,1,0:T(8,128)(2,1)S(1)}, u32[]{:S(2)}) copy-start(bf16[5,64,1536]{2,1,0:T(8,128)(2,1)S(1)} %get-tuple-element.9) | copy-start | bytes 2949124
  664.7 4.4 copy-start.1
  672.9 367.4 %reduce-scatter.3.cloned.1.call-start = ((), (), s32[]{:S(2)}) async-start(), calls=%async_computation.5 | async-start | bytes 14598144 | tf_op jit(solution)/shard_map/reduce_scatter | solution.py:102
  673.1 1.2 copy-start.2
  674.3 3.0 copy-start.5
  677.3 3.6 copy-start.4
  699.2 425.0 %all-reduce.4.cloned.1.call-start = ((), (), s32[]{:S(2)}) async-start(), calls=%async_computation.8 | async-start | bytes 1179648 | tf_op jit(solution)/shard_map/psum | solution.py:114
Sparse Core Ops, SparseCore 0:
  9.6 140.4 all-gather.9
  151.8 164.4 all-gather.5
  318.0 214.3 all-gather.11
  533.9 130.7 all-gather.7
  673.0 170.2 reduce-scatter.4
  845.6 194.5 reduce-scatter.2
  1042.8 60.5 all-reduce.3
